TPU v7x, 32 devices: a whole 2x2x4 slice. The times are simulated.
32 devices in a mesh: seq: 8 (over z, x), tp: 4 (over y, core).
Axes of the slice: x: 2, y: 2, z: 4, core: 2. Of those that a mesh axis runs over, the one named last changes fastest.
Arguments:
- mixer_input: bfloat16 [2048, 16384], P('seq', 'tp'), may hold values from -512 to 512
- mixer_gate: bfloat16 [2048, 16384], P('seq', 'tp'), may hold values from -5 to 5
- state_write: bfloat16 [2048, 128], P('seq'), may hold values from -6 to 6
- state_read: bfloat16 [2048, 128], P('seq'), may hold values from -0.5 to 0.5
- log_decay: float32 [128, 2048], P('tp', 'seq'), may hold values from -1 to 0
- norm_gain: float32 [16384], P('tp'), may hold values from 0.1 to 1.9
- queries: bfloat16 [2048, 8192], P('seq', 'tp'), may hold values from -25 to 25
- key_matrix_rows: bfloat16 [2048, 1024], P('seq', 'tp'), may hold values from -25 to 25
- value_matrix_rows: bfloat16 [2048, 1024], P('seq', 'tp'), may hold values from -6 to 6
- request_blocks: int32 [4], replicated, may hold values from 1 to 8, as said below
Outputs:
- mixer_out: bfloat16 [2048, 16384], P('seq', 'tp')
- attention_out: bfloat16 [2048, 8192], P('seq', 'tp')
Inputs may be any that keep to these rules, and one draw needn't show every extreme that they name: `request_blocks`: requests are packed in order and fill the sequence; the second request holds exactly 8 blocks.
All inputs are finite; a program needn't handle non-finite values.
Results may differ from a plain program's by a relative error of at most 0.011.
Values may be sent and summed in bfloat16 or wider, within the bound.
A program may use at most 128 MiB of HBM per device.

v0:
```python
from functools import partial
import math

import jax
import jax.numpy as jnp
from jax import lax
from jax.sharding import PartitionSpec as P

HEADS = 128
P_SIZE = 128
N = 128
QUERY_HEAD_COUNT = 64
KEY_VALUE_HEADS = 8
HEAD_WIDTH = 128
CYCLE = 4


def from_behind(shard, axis, by):
    length = lax.axis_size(axis)
    pairs = [(i, i + by) for i in range(length) if 0 <= i + by < length]
    return lax.ppermute(shard, axis, pairs)


def entering_2(shard, axis, join, neutral):
    place = lax.axis_index(axis)
    gathered = jax.tree.map(
        lambda a, kind: lax.all_gather(a.astype(kind), axis), shard, (jnp.bfloat16, jnp.bfloat16)
    )
    state = jax.tree.map(lambda a, e: jnp.zeros_like(a) + jnp.asarray(e, a.dtype), shard, neutral)

    def one(hop, state):
        return join(
            state,
            jax.tree.map(
                lambda a, own: lax.dynamic_index_in_dim(a, hop, 0, False).astype(own.dtype),
                gathered,
                shard,
            ),
        )

    return lax.fori_loop(0, place, one, state)


def segment_ids(request_blocks, positions):
    request_ends = jnp.cumsum(request_blocks) * 128
    counted = jnp.sum((positions[:, None] >= request_ends[None, :]).astype(jnp.int32), axis=1)
    return jnp.where(positions < 0, -1, counted)


def combine_states(first_part, second_part):
    return (
        first_part[0] * second_part[0],
        second_part[0][:, None, None] * first_part[1] + second_part[1],
    )


def local_terms(mixer_input, state_write, state_read, log_decay, segment, segment_before):
    row_count = mixer_input.shape[0]
    head_count = log_decay.shape[0]
    block_count = row_count // 128
    inputs = mixer_input.reshape(block_count, 128, head_count, P_SIZE)
    writes = state_write.reshape(block_count, 128, N)
    read_rows = state_read.reshape(block_count, 128, N)
    running = jnp.cumsum(log_decay.reshape(head_count, block_count, 128), axis=2).transpose(1, 0, 2)
    labels = segment.reshape(block_count, 128)
    before = jnp.concatenate([segment_before[None], labels[:-1, -1]])
    causal = jnp.tril(jnp.ones((128, 128), dtype=bool))
    shared = ((labels[:, :, None] == labels[:, None, :]) & causal[None])[:, None]
    spread = jnp.where(shared, running[:, :, :, None] - running[:, :, None, :], 0.0)
    weight = jnp.where(shared, jnp.exp(spread), 0.0)
    affinity = jnp.einsum("bin,bjn->bij", read_rows, writes, preferred_element_type=jnp.float32)
    mixing = (weight * affinity[:, None]).astype(jnp.bfloat16)
    within = jnp.einsum("bhij,bjhp->bihp", mixing, inputs, preferred_element_type=jnp.float32)
    reaching = jnp.where(
        (labels == labels[:, -1:])[:, None, :], jnp.exp(running[:, :, -1:] - running), 0.0
    )
    carried = (inputs * reaching.transpose(0, 2, 1)[:, :, :, None]).astype(jnp.bfloat16)
    block_state = jnp.einsum("bjn,bjhp->bhnp", writes, carried, preferred_element_type=jnp.float32)
    opened = labels == before[:, None]
    entry_decay = jnp.where(opened[:, None, :], jnp.exp(running), 0.0)
    block_decay = jnp.where(opened[:, -1:], jnp.exp(running[:, :, -1]), 0.0)
    running_state = jnp.zeros((head_count, N, P_SIZE), jnp.float32)
    factor = jnp.ones((head_count,), jnp.float32)
    entering_list = []
    factor_list = []
    for block_index in range(block_count):
        entering_list.append(running_state)
        factor_list.append(factor)
        running_state = (
            block_decay[block_index][:, None, None] * running_state + block_state[block_index]
        )
        factor = factor * block_decay[block_index]
    return (
        within,
        read_rows,
        entry_decay,
        jnp.stack(entering_list),
        jnp.stack(factor_list),
        factor,
        running_state,
    )


def absorb(
    carry,
    query_heads,
    moving_pair,
    query_segment,
    query_positions,
    key_segment,
    key_positions,
    scale,
):
    largest, totals, summed = carry
    key_heads = query_heads.shape[1]
    key_part = moving_pair[0].reshape(-1, key_heads, HEAD_WIDTH)
    value_part = moving_pair[1].reshape(-1, key_heads, HEAD_WIDTH)
    scores = (
        jnp.einsum("tkgd,skd->kgts", query_heads, key_part, preferred_element_type=jnp.float32)
        * scale
    )
    allowed = (query_segment[:, None] == key_segment[None, :]) & (
        key_positions[None, :] <= query_positions[:, None]
    )
    masked = jnp.where(allowed[None, None], scores, -jnp.inf)
    new_largest = jnp.maximum(largest, jnp.max(masked, axis=3))
    weights = jnp.exp(masked - new_largest[..., None])
    rescale = jnp.exp(largest - new_largest)
    totals = totals * rescale + jnp.sum(weights, axis=3)
    rounded = weights.astype(jnp.bfloat16)
    summed = summed * rescale.transpose(2, 0, 1)[..., None] + jnp.einsum(
        "kgts,skd->tkgd", rounded, value_part, preferred_element_type=jnp.float32
    )
    return (new_largest, totals, summed)


def attention_part(queries, key_matrix_rows, value_matrix_rows, request_blocks, positions, segment):
    row_count = queries.shape[0]
    key_heads = key_matrix_rows.shape[1] // HEAD_WIDTH
    query_group = QUERY_HEAD_COUNT // KEY_VALUE_HEADS
    query_heads = queries.reshape(row_count, key_heads, query_group, HEAD_WIDTH)
    scale = 1.0 / math.sqrt(HEAD_WIDTH)
    own_pair = jnp.stack([key_matrix_rows, value_matrix_rows])
    carry = (
        jnp.full((key_heads, query_group, row_count), -jnp.inf, jnp.float32),
        jnp.zeros((key_heads, query_group, row_count), jnp.float32),
        jnp.zeros((row_count, key_heads, query_group, HEAD_WIDTH), jnp.float32),
    )
    carry = absorb(carry, query_heads, own_pair, segment, positions, segment, positions, scale)
    moving = own_pair
    for step in range(1, CYCLE + 1):
        moving = from_behind(moving, "seq", 1)
        key_positions = positions - step * row_count
        key_segment = segment_ids(request_blocks, key_positions)
        update = partial(
            absorb,
            query_heads=query_heads,
            moving_pair=moving,
            query_segment=segment,
            query_positions=positions,
            key_segment=key_segment,
            key_positions=key_positions,
            scale=scale,
        )
        carry = update(carry)
    largest, totals, summed = carry
    result = summed / totals.transpose(2, 0, 1)[..., None]
    return result.reshape(row_count, key_heads * query_group * HEAD_WIDTH).astype(jnp.bfloat16)


def on_device(
    mixer_input,
    mixer_gate,
    state_write,
    state_read,
    log_decay,
    norm_gain,
    queries,
    key_matrix_rows,
    value_matrix_rows,
    request_blocks,
):
    row_count = mixer_input.shape[0]
    head_count = log_decay.shape[0]
    positions = lax.axis_index("seq") * row_count + lax.iota(jnp.int32, row_count)
    segment = segment_ids(request_blocks, positions)
    segment_before = segment_ids(request_blocks, positions[:1] - 1)[0]
    within, read_rows, entry_decay, entering_local, factor_local, decay_all, state_all = (
        local_terms(mixer_input, state_write, state_read, log_decay, segment, segment_before)
    )
    identity = (jnp.ones_like(decay_all), jnp.zeros_like(state_all))
    scanned = entering_2((decay_all, state_all), "seq", combine_states, identity)
    entering = scanned[1]
    attention_out = attention_part(
        queries, key_matrix_rows, value_matrix_rows, request_blocks, positions, segment
    )
    states_in = entering_local + factor_local[:, :, None, None] * entering[None]
    from_state = jnp.einsum(
        "bin,bhnp->bihp", read_rows.astype(jnp.float32), states_in, precision=lax.Precision.HIGHEST
    )
    mixed = within + from_state * entry_decay.transpose(0, 2, 1)[:, :, :, None]
    gated = mixed.reshape(row_count, head_count, P_SIZE) * jax.nn.silu(
        mixer_gate.astype(jnp.float32).reshape(row_count, head_count, P_SIZE)
    )
    squares = lax.psum(jnp.sum(gated * gated, axis=(1, 2)), "tp")
    scaling = lax.rsqrt(squares / (HEADS * P_SIZE) + 1e-05)
    mixer_out = (gated * scaling[:, None, None]).reshape(
        row_count, head_count * P_SIZE
    ) * norm_gain[None, :]
    return (mixer_out.astype(jnp.bfloat16), attention_out)


def solution(mesh):
    placed = (
        P("seq", "tp"),
        P("seq", "tp"),
        P("seq", None),
        P("seq", None),
        P("tp", "seq"),
        P("tp"),
        P("seq", "tp"),
        P("seq", "tp"),
        P("seq", "tp"),
        P(),
    )
    return jax.shard_map(
        on_device,
        mesh=mesh,
        in_specs=placed,
        out_specs=(P("seq", "tp"), P("seq", "tp")),
        check_vma=False,
    )
```

profile of v0, /device:TPU:26, one launch (start us, length us, event | category | flops | bytes accessed | tf_op | source)
XLA Modules:
  0.0 213.5 jit_solution(14712242026973353004)
XLA Ops:
  12.4 3.4 %copy.176 = bf16[32,8,32,128]{3,2,1,0:T(8,128)(2,1)} copy(bf16[32,8,32,128]{3,1,2,0:T(8,128)(2,1)} %bitcast.323) | data formatting | bytes 4194304
  15.8 3.5 %copy.120 = bf16[2,128,32,128]{1,3,2,0:T(8,128)(2,1)S(1)} copy(bf16[2,128,32,128]{3,2,1,0:T(8,128)(2,1)} %bitcast.322) | data formatting | bytes 4194304 | tf_op jit(solution)/shard_map/reshape | solution.py:61
  22.8 1.8 fusion.37
  34.1 2.5 %convert_bitcast_fusion = f32[32,8,32,128]{3,1,2,0:T(8,128)} fusion(bf16[256,4096]{1,0:T(8,128)(2,1)S(1)} %copy-done.2), kind=kLoop, calls=%fused_computation.2 | loop fusion | flops 1048576 | bytes 6291456
  38.5 17.2 %all-gather = bf16[8,1,32]{2,1,0:T(2,128)(2,1)S(1)} all-gather(bf16[1,1,32]{2,1,0:T(2,128)(2,1)} %get-tuple-element.117), channel_id=1, replica_groups=mesh['seq'=8,'tp'=4] {'seq'}, dimensions={0}, use_global_device_ids=true | all-gather | bytes 576 | tf_op jit(solution)/shard_map/all_gather | solution.py:27
  56.3 4.9 %copy.178 = f32[32,8,32,128]{3,2,1,0:T(8,128)} copy(f32[32,8,32,128]{3,1,2,0:T(8,128)} %convert_bitcast_fusion) | data formatting | bytes 8388608
  61.2 5.4 %copy.126 = f32[2,128,32,128]{1,3,2,0:T(8,128)} copy(f32[2,128,32,128]{3,2,1,0:T(8,128)} %bitcast.321) | data formatting | bytes 8388608 | tf_op jit(solution)/shard_map/reshape | solution.py:203
  71.3 5.2 %collective-permute-done.1 = bf16[2,256,256]{1,2,0:T(8,128)(2,1)S(1)} collective-permute-done((bf16[2,256,256]{1,2,0:T(8,128)(2,1)}, bf16[2,256,256]{1,2,0:T(8,128)(2,1)S(1)}, u32[]{:S(2)}, u32[]{:S(2)}) %collective-permute-start.1) | collective-permute-done | bytes 262176 | tf_op jit(solution)/shard_map/ppermute | solution.py:21
  78.8 12.9 %collective-permute-done.2 = bf16[2,256,256]{1,2,0:T(8,128)(2,1)S(1)} collective-permute-done((bf16[2,256,256]{1,2,0:T(8,128)(2,1)S(1)}, bf16[2,256,256]{1,2,0:T(8,128)(2,1)S(1)}, u32[]{:S(2)}, u32[]{:S(2)}) %collective-permute-start.2) | collective-permute-done | bytes 262176 | tf_op jit(solution)/shard_map/ppermute | solution.py:21
  94.1 21.4 %collective-permute-done.3 = bf16[2,256,256]{1,2,0:T(8,128)(2,1)S(1)} collective-permute-done((bf16[2,256,256]{1,2,0:T(8,128)(2,1)S(1)}, bf16[2,256,256]{1,2,0:T(8,128)(2,1)S(1)}, u32[]{:S(2)}, u32[]{:S(2)}) %collective-permute-start.3) | collective-permute-done | bytes 262176 | tf_op jit(solution)/shard_map/ppermute | solution.py:21
  123.5 1.9 fusion.39
  126.8 32.5 %all-gather.3.cloned.1.call-done = bf16[8,32,128,128]{3,2,1,0:T(8,128)(2,1)} async-done(((bf16[1,32,128,128]{3,2,1,0:T(8,128)(2,1)}), bf16[8,32,128,128]{3,2,1,0:T(8,128)(2,1)}) %all-gather.3.cloned.1.call-update) | async-done | bytes 8388624 | tf_op jit(solution)/shard_map/all_gather | solution.py:27
  159.6 16.8 %while.12 = (s32[]{:T(128)}, f32[32,128,128]{2,1,0:T(8,128)S(1)}, s32[]{:T(128)}, bf16[8,32]{1,0:T(8,128)(2,1)}, bf16[8,32,128,128]{3,2,1,0:T(8,128)(2,1)}, /*index=5*/s32[]{:T(128)}, s32[]{:T(128)}, s32[]{:T(128)}) while((s32[]{:T(128)}, f32[32,128,128]{2,1,0:T(8,128)S(1)}, s32[]{:T(128)}, bf16[8,32]{1,0:T(8,128)(2,1)}, ...), condition=%wide.region_5.6_spmd, body=%wide.region_4.5_spmd.sunk | while | flops 1572901 | bytes 5243327 | solution.py:41
  160.3 1.7 convert_add_fusion.2
  162.6 1.7 convert_add_fusion.2
  165.0 1.7 convert_add_fusion.2
  167.4 1.7 convert_add_fusion.2
  169.7 1.7 convert_add_fusion.2
  176.4 1.9 copy.123
  178.3 4.8 %fusion.7 = f32[2,32,128,128]{3,2,1,0:T(8,128)S(1)} fusion(bf16[2,128,128,1]{2,1,3,0:T(8,128)(2,1)S(1)} %bitcast.340, f32[1,32,128,128]{2,3,1,0:T(8,128)} %get-tuple-element.97, f32[32,128,128]{1,2,0:T(8,128)} %copy.123, f32[2,32]{1,0:T(2,128)S(1)} %copy-done.20), kind=kOutput, calls=%fused_computation.24 | convolution fusion | flops 1612709888 | bytes 8454400 | tf_op jit(solution)/shard_map/bin,bhnp->bihp/dot_general | solution.py:198
  183.1 4.2 %multiply_reduce_fusion = (f32[2,128]{1,0:T(2,128)S(1)}, f32[2,128,32,128]{1,3,2,0:T(8,128)}) fusion(f32[2,128,32,128]{1,3,2,0:T(8,128)S(1)} %copy-done.6, f32[2,128,32]{1,2,0:T(8,128)S(1)} %copy-done.15, f32[2,32,128,128]{3,2,1,0:T(8,128)S(1)} %fusion.7, bf16[2,128,32,128]{1,3,2,0:T(8,128)(2,1)S(1)} %copy-done.5, f32[2,128,128]{2,1,0:T(8,128)S(1)} %copy-done.13, ...), kind=kOutput, calls=%fused_computation.23 | convolution fusion | flops 283115264 | bytes 14910464 | tf_op jit(solution)/shard_map/bhij,bjhp->bihp/dot_general | solution.py:73
  187.3 5.6 %copy.124 = f32[2,128,32,128]{3,2,1,0:T(8,128)} copy(f32[2,128,32,128]{1,3,2,0:T(8,128)} %get-tuple-element.123) | data formatting | bytes 8388608 | tf_op jit(solution)/shard_map/add | solution.py:201
  192.9 6.1 %psum.7 = f32[256]{0:T(256)S(1)} all-reduce(f32[256]{0:T(256)S(1)} %bitcast.343), channel_id=1, replica_groups=mesh['seq'=8,'tp'=4] {'tp'}, use_global_device_ids=true, to_apply=%region_7.8 | all-reduce | flops 256 | bytes 2048 | tf_op jit(solution)/shard_map/psum | solution.py:205
  199.1 7.6 %fusion.11 = bf16[256,4096]{1,0:T(8,128)(2,1)} fusion(bf16[256,4096]{1,0:T(8,128)(2,1)S(1)} %copy-done.3, f32[32,8,32,128]{3,2,1,0:T(8,128)} %bitcast.320, f32[4096]{0:T(1024)S(1)} %copy-done.17, f32[256]{0:T(256)S(1)} %add_rsqrt_fusion), kind=kLoop, calls=%fused_computation.30 | loop fusion | flops 9437184 | bytes 8406016 | tf_op jit(solution)/shard_map/convert_element_type | solution.py:210
  (124 shorter events, 46.4 us)
Async XLA Ops:
  7.2 15.0 %copy-start = (bf16[256,128]{1,0:T(8,128)(2,1)S(1)}, bf16[256,128]{1,0:T(8,128)(2,1)}, u32[]{:S(2)}) copy-start(bf16[256,128]{1,0:T(8,128)(2,1)} %param.14) | copy-start | bytes 196612
  7.2 152.1 %all-gather.3.cloned.1.call-start = ((), (), s32[]{:S(2)}) async-start(), calls=%async_computation | async-start | bytes 9437184 | tf_op jit(solution)/shard_map/all_gather | solution.py:27
  7.3 2.8 %copy-start.21 = (s32[256]{0:T(256)}, s32[256]{0:T(256)S(1)}, u32[]{:S(2)}) copy-start(s32[256]{0:T(256)S(1)} %fusion.99) | copy-start | bytes 3076
  12.2 8.7 %copy-start.9 = (f32[32,2,128]{2,0,1:T(8,128)}, f32[32,2,128]{2,0,1:T(8,128)S(1)}, u32[]{:S(2)}) copy-start(f32[32,2,128]{2,0,1:T(8,128)S(1)} %reduce_window_sum.23) | copy-start | bytes 98308
  19.3 5.3 %copy-start.4 = (bf16[2,128,32,128]{1,3,2,0:T(8,128)(2,1)}, bf16[2,128,32,128]{1,3,2,0:T(8,128)(2,1)S(1)}, u32[]{:S(2)}) copy-start(bf16[2,128,32,128]{1,3,2,0:T(8,128)(2,1)S(1)} %copy.120) | copy-start | bytes 6291460
  22.8 4.1 %copy-start.8 = (bf16[256,256]{1,0:T(8,128)(2,1)S(1)}, bf16[256,256]{1,0:T(8,128)(2,1)}, u32[]{:S(2)}) copy-start(bf16[256,256]{1,0:T(8,128)(2,1)} %param.19) | copy-start | bytes 393220
  24.6 6.1 %copy-start.22 = (s32[256]{0:T(256)S(1)}, s32[256]{0:T(256)}, u32[]{:S(2)}) copy-start(s32[256]{0:T(256)} %copy-done.21) | copy-start | bytes 3076
  27.8 40.2 %collective-permute-start = (bf16[2,256,256]{1,2,0:T(8,128)(2,1)}, bf16[2,256,256]{1,2,0:T(8,128)(2,1)}, u32[]{:S(2)}, u32[]{:S(2)}) collective-permute-start(bf16[2,256,256]{1,2,0:T(8,128)(2,1)} %pad_maximum_fusion), channel_id=1, source_target_pairs={{0,4},{4,8},{8,12},{12,16},{16,20},{20,24},{24,28},{1,5},{5,9},{9,... | collective-permute-start | bytes 786440 | tf_op jit(solution)/shard_map/ppermute | solution.py:21
  31.8 2.4 %copy-start.2 = (bf16[256,4096]{1,0:T(8,128)(2,1)S(1)}, bf16[256,4096]{1,0:T(8,128)(2,1)}, u32[]{:S(2)}) copy-start(bf16[256,4096]{1,0:T(8,128)(2,1)} %param.13) | copy-start | bytes 6291460
  61.2 5.4 %copy-start.23 = (f32[1,32]{1,0:T(1,128)S(1)}, f32[1,32]{1,0:T(1,128)}, u32[]{:S(2)}) copy-start(f32[1,32]{1,0:T(1,128)} %get-tuple-element.114) | copy-start | bytes 388
  61.2 6.0 %copy-start.11 = (bf16[256,128]{1,0:T(8,128)(2,1)S(1)}, bf16[256,128]{1,0:T(8,128)(2,1)}, u32[]{:S(2)}) copy-start(bf16[256,128]{1,0:T(8,128)(2,1)} %param.15) | copy-start | bytes 196612
  68.0 8.5 %collective-permute-start.1 = (bf16[2,256,256]{1,2,0:T(8,128)(2,1)}, bf16[2,256,256]{1,2,0:T(8,128)(2,1)S(1)}, u32[]{:S(2)}, u32[]{:S(2)}) collective-permute-start(bf16[2,256,256]{1,2,0:T(8,128)(2,1)} %collective-permute-done), channel_id=1, source_target_pairs={{0,4},{4,8},{8,12},{12,16},{16,20},{20,24},{24,28},{1,5},{5,9},{9,... | collective-permute-start | bytes 786440 | tf_op jit(solution)/shard_map/ppermute | solution.py:21
  76.5 15.2 %collective-permute-start.2 = (bf16[2,256,256]{1,2,0:T(8,128)(2,1)S(1)}, bf16[2,256,256]{1,2,0:T(8,128)(2,1)S(1)}, u32[]{:S(2)}, u32[]{:S(2)}) collective-permute-start(bf16[2,256,256]{1,2,0:T(8,128)(2,1)S(1)} %collective-permute-done.1), channel_id=1, source_target_pairs={{0,4},{4,8},{8,12},{12,16},{16,20},{20,24},{24,28},{1,5},{5,9},{9,... | collective-permute-start | bytes 786440 | tf_op jit(solution)/shard_map/ppermute | solution.py:21
  78.8 36.8 %copy-start.7 = (pred[256,256]{0,1:T(8,128)(4,1)S(1)}, pred[256,256]{0,1:T(8,128)(4,1)}, u32[]{:S(2)}) copy-start(pred[256,256]{0,1:T(8,128)(4,1)} %get-tuple-element.110) | copy-start | bytes 196612
  91.7 23.8 %collective-permute-start.3 = (bf16[2,256,256]{1,2,0:T(8,128)(2,1)S(1)}, bf16[2,256,256]{1,2,0:T(8,128)(2,1)S(1)}, u32[]{:S(2)}, u32[]{:S(2)}) collective-permute-start(bf16[2,256,256]{1,2,0:T(8,128)(2,1)S(1)} %collective-permute-done.2), channel_id=1, source_target_pairs={{0,4},{4,8},{8,12},{12,16},{16,20},{20,24},{24,28},{1,5},{5,9},{9,... | collective-permute-start | bytes 786440 | tf_op jit(solution)/shard_map/ppermute | solution.py:21
  178.2 4.8 %copy-start.5 = (bf16[2,128,32,128]{1,3,2,0:T(8,128)(2,1)S(1)}, bf16[2,128,32,128]{1,3,2,0:T(8,128)(2,1)}, u32[]{:S(2)}) copy-start(bf16[2,128,32,128]{1,3,2,0:T(8,128)(2,1)} %copy-done.4) | copy-start | bytes 6291460
  178.2 4.8 %copy-start.6 = (f32[2,128,32,128]{1,3,2,0:T(8,128)S(1)}, f32[2,128,32,128]{1,3,2,0:T(8,128)}, u32[]{:S(2)}) copy-start(f32[2,128,32,128]{1,3,2,0:T(8,128)} %copy.126) | copy-start | bytes 12582916
  178.2 4.8 %copy-start.10 = (f32[32,2,128]{2,0,1:T(8,128)S(1)}, f32[32,2,128]{2,0,1:T(8,128)}, u32[]{:S(2)}) copy-start(f32[32,2,128]{2,0,1:T(8,128)} %copy-done.9) | copy-start | bytes 98308
  178.2 4.8 %copy-start.13 = (f32[2,128,128]{2,1,0:T(8,128)S(1)}, f32[2,128,128]{2,1,0:T(8,128)}, u32[]{:S(2)}) copy-start(f32[2,128,128]{2,1,0:T(8,128)} %fusion.121) | copy-start | bytes 393220
  178.2 4.8 %copy-start.15 = (f32[2,128,32]{1,2,0:T(8,128)S(1)}, f32[2,128,32]{1,2,0:T(8,128)}, u32[]{:S(2)}) copy-start(f32[2,128,32]{1,2,0:T(8,128)} %get-tuple-element.106) | copy-start | bytes 98308
  178.3 4.8 %copy-start.16 = (pred[2,128,128]{2,1,0:T(8,128)(4,1)S(1)}, pred[2,128,128]{2,1,0:T(8,128)(4,1)}, u32[]{:S(2)}) copy-start(pred[2,128,128]{2,1,0:T(8,128)(4,1)} %compare_and_fusion.5) | copy-start | bytes 98308
  187.3 11.8 %copy-start.3 = (bf16[256,4096]{1,0:T(8,128)(2,1)S(1)}, bf16[256,4096]{1,0:T(8,128)(2,1)}, u32[]{:S(2)}) copy-start(bf16[256,4096]{1,0:T(8,128)(2,1)} %param.13) | copy-start | bytes 6291460
  187.3 11.8 %copy-start.17 = (f32[4096]{0:T(1024)S(1)}, f32[4096]{0:T(1024)}, u32[]{:S(2)}) copy-start(f32[4096]{0:T(1024)} %param.17) | copy-start | bytes 49156
  199.0 7.6 %copy-start.1 = (bf16[256,128]{1,0:T(8,128)(2,1)S(1)}, bf16[256,128]{1,0:T(8,128)(2,1)}, u32[]{:S(2)}) copy-start(bf16[256,128]{1,0:T(8,128)(2,1)} %param.14) | copy-start | bytes 196612
  (5 other events, 8.9 us)
Sparse Core Ops, SparseCore 0:
  26.1 133.2 all-gather.2
where the time goes:
time: 215 us; the launch traced here: 213 us
  waiting for transfers between devices  72 us (33%)
  other arithmetic  39.9 us (19%)
  local copies, waits for them, and re-layouts  35 us (16%)
  blocking collectives  23.3 us (11%)
  matrix products  21.7 us (10%)
  between operations  15.8 us (7%)
  starting transfers between devices  5.34 us (2%)
    ppermute x4, waiting for transfers between devices, from_behind(): return lax.ppermute(shard, axis, pairs)  39.5 us
    all_gather x1, waiting for transfers between devices, entering_2(): lax.all_gather(a.astype(kind), axis)  32.5 us
    all_gather x1, blocking collectives, entering_2(): lax.all_gather(a.astype(kind), axis)  17.2 us
    unnamed x54, local copies, waits for them, and re-layouts  12 us
    add x7, other arithmetic, combine_states(): second_part[0][:, None, None] * first_part[1] + second_part[1]  11.6 us
    convert_element_type x1, other arithmetic, on_device(): return (mixer_out.astype(jnp.bfloat16), attention_out)  7.6 us
    dot_general x5, matrix products, absorb(): jnp.einsum('kgts,skd->tkgd', rounded, value_part, preferred_element_type=...  6.44 us
    psum x1, blocking collectives, on_device(): squares = lax.psum(jnp.sum(gated * gated, axis=(1, 2)), 'tp')  6.1 us
  transfers between devices with their start and end apart: 5, of which 4 were waited for; matrix products, arithmetic and copies ran while one was open for 18% of the time, Pallas kernels for 0%

commit v1 on v0

v1 whole, which is shorter than its diff:
```python
from functools import partial
import math

import jax
import jax.numpy as jnp
from jax import lax
from jax.experimental import pallas as pl
from jax.experimental.pallas import tpu as pltpu
from jax.sharding import PartitionSpec as P

WIDTH = 128
BLOCK = 128
CYCLE = 4
CHUNK = 4
FAR = -1e30
MESH = pl.DeviceIdType.MESH
HIGH = lax.Precision.HIGHEST


def lanes(h):
    return pl.ds(pl.multiple_of(h * WIDTH, WIDTH), WIDTH)


def dot_t(a, b, precision=None):
    return lax.dot_general(
        a, b, (((1,), (1,)), ((), ())), preferred_element_type=jnp.float32, precision=precision
    )


def dot(a, b, precision=None):
    return jnp.dot(a, b, preferred_element_type=jnp.float32, precision=precision)


def kernel(
    n_seq, n_tp, features,
    rb, x_ref, g_ref, b_ref, c_ref, ld_ref, gain_ref, q_ref, k_ref, v_ref,
    out_ref, att_ref,
    kv, bias, run, colb, bt, aff, wbuf, s0, slab, partner_s, ent, ent_own, eout,
    gdec, gpart, sq, ss, ssbuf,
    kv_send, kv_recv, st_send, st_recv, ev_send, e_recv, ch_send, gd_sem, ss_send, ss_recv,
):
    d = lax.axis_index("seq")
    t = lax.axis_index("tp")
    odd = lax.rem(d, 2)
    is_odd = odd == 1
    is_even = odd == 0
    partner = d + 1 - 2 * odd
    has_next = d + 2 < n_seq
    has_prev = d >= 2
    rows = x_ref.shape[0]
    heads = ld_ref.shape[0]
    q_heads = q_ref.shape[1] // WIDTH
    kv_heads = k_ref.shape[1] // WIDTH
    group = q_heads // kv_heads
    chunks = heads // CHUNK
    half = (slice(0, BLOCK), slice(BLOCK, 2 * BLOCK))

    barrier = pltpu.get_barrier_semaphore()
    pl.semaphore_signal(barrier, inc=1, device_id={"seq": partner}, device_id_type=MESH)
    for r in range(1, n_tp):
        pl.semaphore_signal(
            barrier, inc=1, device_id={"tp": lax.rem(t + r, n_tp)}, device_id_type=MESH
        )

    @pl.when(has_next)
    def _():
        pl.semaphore_signal(barrier, inc=1, device_id={"seq": d + 2}, device_id_type=MESH)

    @pl.when(has_prev)
    def _():
        pl.semaphore_signal(barrier, inc=1, device_id={"seq": d - 2}, device_id_type=MESH)

    peers = n_tp + has_next.astype(jnp.int32) + has_prev.astype(jnp.int32)
    pl.semaphore_wait(barrier, peers)

    def kv_copy(part, source, send, slot, target):
        own = (k_ref, v_ref)[part]
        return pltpu.make_async_remote_copy(
            src_ref=own if source is None else kv.at[source, part],
            dst_ref=kv.at[slot, part],
            send_sem=kv_send.at[send, part],
            recv_sem=kv_recv.at[slot, part],
            device_id={"seq": target},
            device_id_type=MESH,
        )

    own_up = (has_next, None, 0, 1, d + 2)
    own_side = (is_even, None, 1, 0, d + 1)
    relay_up = (has_prev & has_next, 1, 2, 3, d + 2)
    relay_even = (has_prev & is_even, 1, 1 + 2, 2, d + 1)
    relay_odd = (has_prev & is_odd, 1, 1 + 2, 0, d - 1)
    last_odd = ((d >= 4) & is_odd, 3, 4, 2, d - 1)

    def start(move):
        @pl.when(move[0])
        def _():
            for part in range(2):
                kv_copy(part, *move[1:]).start()

    def sent(move):
        @pl.when(move[0])
        def _():
            for part in range(2):
                kv_copy(part, *move[1:]).wait_send()

    def arrived(slot):
        @pl.when(d >= slot + 1)
        def _():
            for part in range(2):
                kv_copy(part, None, 0, slot, partner).wait_recv()

    start(own_up)
    start(own_side)
    for slot in range(CYCLE):
        @pl.when(d < slot + 1)
        def _():
            kv[slot] = jnp.zeros(kv.shape[1:], kv.dtype)

    @pl.when(d < 2)
    def _():
        ent[...] = jnp.zeros(ent.shape, ent.dtype)

    ends = []
    total = jnp.int32(0)
    for i in range(4):
        total = total + rb[i]
        ends.append(total)

    def opened(block):
        flag = jnp.where(block == 0, 0.0, 1.0)
        for e in ends:
            flag = flag * jnp.where(block == e, 0.0, 1.0)
        return flag

    open_0 = opened(2 * d)
    open_1 = opened(2 * d + 1)
    opens = (open_0, open_1)

    i_r = lax.broadcasted_iota(jnp.int32, (rows, rows), 0)
    i_c = lax.broadcasted_iota(jnp.int32, (rows, rows), 1)
    lower = jnp.where((i_c <= i_r) & (i_r // BLOCK == i_c // BLOCK), 1.0, 0.0)
    decays = ld_ref[...]
    sums_row = dot_t(decays, lower, HIGH)
    columns = dot_t(lower, decays, HIGH)
    for h in range(heads):
        colb[h] = jnp.broadcast_to(columns[:, h : h + 1], (rows, WIDTH))
        run[h] = sums_row[h : h + 1, :]
        gdec[h] = open_0 * open_1 * jnp.exp(
            colb[h, BLOCK - 1 : BLOCK, :] + colb[h, 2 * BLOCK - 1 : 2 * BLOCK, :]
        )

    def decay_copy():
        return pltpu.make_async_remote_copy(
            src_ref=gdec, dst_ref=gpart, send_sem=gd_sem.at[0], recv_sem=gd_sem.at[1],
            device_id={"seq": partner}, device_id_type=MESH,
        )

    @pl.when(is_even)
    def _():
        decay_copy().start()

    bt[...] = b_ref[...].astype(jnp.float32).T.astype(jnp.bfloat16)

    def part_of(ref, c):
        return ref.at[pl.ds(c * CHUNK, CHUNK)]

    def slab_copy(c):
        return pltpu.make_async_remote_copy(
            src_ref=part_of(slab, c), dst_ref=part_of(partner_s, c),
            send_sem=st_send.at[c], recv_sem=st_recv.at[c],
            device_id={"seq": partner}, device_id_type=MESH,
        )

    def side_copy(c):
        return pltpu.make_async_remote_copy(
            src_ref=part_of(ent, c), dst_ref=part_of(ent, c),
            send_sem=ev_send.at[c], recv_sem=e_recv.at[c],
            device_id={"seq": d - 1}, device_id_type=MESH,
        )

    def chain_copy(c):
        return pltpu.make_async_remote_copy(
            src_ref=part_of(eout, c), dst_ref=part_of(ent, c),
            send_sem=ch_send.at[c], recv_sem=e_recv.at[c],
            device_id={"seq": d + 2}, device_id_type=MESH,
        )

    def state_of(h):
        states = []
        for b in range(2):
            last_row = colb[h, b * BLOCK + BLOCK - 1 : b * BLOCK + BLOCK, :]
            reach = jnp.exp(last_row - colb[h, half[b], :])
            carried = (x_ref[half[b], lanes(h)].astype(jnp.float32) * reach).astype(jnp.bfloat16)
            states.append(dot(bt[:, half[b]], carried))
        g_1 = open_1 * jnp.exp(colb[h, 2 * BLOCK - 1 : 2 * BLOCK, :])
        s0[h] = states[0].astype(jnp.bfloat16)
        slab[h] = (g_1 * states[0] + states[1]).astype(jnp.bfloat16)

    def state_chunk(c, carry):
        for i in range(CHUNK):
            state_of(c * CHUNK + i)

        @pl.when(is_even)
        def _():
            slab_copy(c).start()

        return carry

    lax.fori_loop(0, chunks, state_chunk, 0)

    arrived(1)
    start(relay_up)
    start(relay_even)
    start(relay_odd)

    for b in range(2):
        aff[b] = dot_t(c_ref[half[b], :], b_ref[half[b], :])
    causal = lax.broadcasted_iota(jnp.int32, (BLOCK, BLOCK), 1) <= lax.broadcasted_iota(
        jnp.int32, (BLOCK, BLOCK), 0
    )

    def within_of(h, carry):
        for b in range(2):
            spread = colb[h, half[b], :] - run[h, :, half[b]]
            weight = jnp.exp(jnp.where(causal, spread, FAR))
            mixing = (weight * aff[b]).astype(jnp.bfloat16)
            wbuf[half[b], lanes(h)] = dot(mixing, x_ref[half[b], lanes(h)])
        return carry

    lax.fori_loop(0, heads, within_of, 0)

    def label(positions):
        found = jnp.zeros(positions.shape, jnp.int32)
        for e in ends:
            found = found + jnp.where(positions >= e * BLOCK, 1, 0)
        return jnp.where(positions < 0, -1, found)

    q_pos = d * rows + lax.broadcasted_iota(jnp.int32, (rows, 1), 0)
    q_label = label(q_pos)
    for slot in range(CYCLE + 1):
        k_pos = (d - slot) * rows + lax.broadcasted_iota(jnp.int32, (1, rows), 1)
        same = (q_label == label(k_pos)) & (k_pos <= q_pos)
        bias[slot] = jnp.where(same, 0.0, FAR)

    arrived(3)
    start(last_odd)
    arrived(0)
    arrived(2)

    @pl.when(is_odd)
    def _():
        decay_copy().wait_recv()

    factor = math.log2(math.e) / math.sqrt(WIDTH)

    def attend(h):
        kh = h // group
        query = q_ref[:, lanes(h)]
        scores = []
        for slot in range(CYCLE + 1):
            key = k_ref[:, lanes(kh)] if slot == 0 else kv[slot - 1, 0, :, lanes(kh)]
            scores.append(dot_t(query, key) + bias[slot])
        top = scores[0]
        for s in scores[1:]:
            top = jnp.maximum(top, s)
        top = jnp.max(top, axis=1, keepdims=True)
        sums = jnp.zeros((rows, rows), jnp.float32)
        result = jnp.zeros((rows, WIDTH), jnp.float32)
        for slot in range(CYCLE + 1):
            value = v_ref[:, lanes(kh)] if slot == 0 else kv[slot - 1, 1, :, lanes(kh)]
            weight = jnp.exp2((scores[slot] - top) * factor)
            sums = sums + weight
            result = result + dot(weight.astype(jnp.bfloat16), value)
        result = result / jnp.sum(sums, axis=1, keepdims=True)
        att_ref[:, lanes(h)] = result.astype(jnp.bfloat16)

    def relay(c):
        slab_copy(c).wait_recv()

        @pl.when(has_prev)
        def _():
            chain_copy(c).wait_recv()
            side_copy(c).start()

        for i in range(CHUNK):
            h = c * CHUNK + i
            own = gpart[h] * ent[h].astype(jnp.float32) + partner_s[h].astype(
                jnp.float32
            )
            ent_own[h] = own.astype(jnp.bfloat16)
            after = gdec[h] * own + slab[h].astype(jnp.float32)
            eout[h] = after.astype(jnp.bfloat16)

        @pl.when(has_next)
        def _():
            chain_copy(c).start()

    per = q_heads // chunks

    def both(c, carry):
        for i in range(per):
            attend(c * per + i)

        @pl.when(is_odd)
        def _():
            relay(c)

        return carry

    lax.fori_loop(0, chunks, both, 0)

    sq[...] = jnp.zeros(sq.shape, jnp.float32)

    def finish_of(h):
        entering = ent_own[h].astype(jnp.float32)
        g_0 = open_0 * jnp.exp(colb[h, BLOCK - 1 : BLOCK, :])
        later = g_0 * entering + s0[h].astype(jnp.float32)
        states = (ent_own[h], later.astype(jnp.bfloat16))
        for b in range(2):
            from_state = dot(c_ref[half[b], :], states[b])
            entry = opens[b] * jnp.exp(colb[h, half[b], :])
            mixed = wbuf[half[b], lanes(h)] + from_state * entry
            gate = g_ref[half[b], lanes(h)].astype(jnp.float32)
            gated = mixed * (gate / (1.0 + jnp.exp(-gate)))
            wbuf[half[b], lanes(h)] = gated
            sq[half[b], :] = sq[half[b], :] + gated * gated

    def finish(c, carry):
        @pl.when(is_even)
        def _():
            @pl.when(has_prev)
            def _():
                side_copy(c).wait_recv()

            ent_own[pl.ds(c * CHUNK, CHUNK)] = ent[pl.ds(c * CHUNK, CHUNK)]

        for i in range(CHUNK):
            finish_of(c * CHUNK + i)
        return carry

    lax.fori_loop(0, chunks, finish, 0)

    ss[...] = dot_t(jnp.ones((8, WIDTH), jnp.float32), sq[...], HIGH)

    def squares_copy(r):
        return pltpu.make_async_remote_copy(
            src_ref=ss, dst_ref=ssbuf.at[r - 1], send_sem=ss_send.at[r - 1],
            recv_sem=ss_recv.at[r - 1], device_id={"tp": lax.rem(t + r, n_tp)},
            device_id_type=MESH,
        )

    for r in range(1, n_tp):
        squares_copy(r).start()
    squares = ss[...]
    for r in range(1, n_tp):
        squares_copy(r).wait_recv()
        squares = squares + ssbuf[r - 1]
    spread_out = lax.dot_general(
        squares, jnp.full((8, WIDTH), 0.125, jnp.float32), (((0,), (0,)), ((), ())),
        preferred_element_type=jnp.float32, precision=HIGH,
    )
    sq[...] = lax.rsqrt(spread_out / features + 1e-05)

    def scale_out(h, carry):
        out_ref[:, lanes(h)] = (
            wbuf[:, lanes(h)] * sq[...] * gain_ref[:, lanes(h)]
        ).astype(jnp.bfloat16)
        return carry

    lax.fori_loop(0, heads, scale_out, 0)

    for r in range(1, n_tp):
        squares_copy(r).wait_send()
    for move in (own_up, own_side, relay_up, relay_even, relay_odd, last_odd):
        sent(move)

    @pl.when(is_even)
    def _():
        decay_copy().wait_send()

    def drain(c, carry):
        @pl.when(is_even)
        def _():
            slab_copy(c).wait_send()

        @pl.when(is_odd & has_prev)
        def _():
            side_copy(c).wait_send()

        @pl.when(is_odd & has_next)
        def _():
            chain_copy(c).wait_send()

        return carry

    lax.fori_loop(0, chunks, drain, 0)


def on_device(n_seq, n_tp, *args):
    (x, gate, write, read, decay, gain, q, k, v, request_blocks) = args
    rows = x.shape[0]
    heads = decay.shape[0]
    chunks = heads // CHUNK
    f32, bf16 = jnp.float32, jnp.bfloat16
    states = pltpu.VMEM((heads, WIDTH, WIDTH), bf16)
    dma = pltpu.SemaphoreType.DMA
    vmem = pl.BlockSpec(memory_space=pltpu.VMEM)
    return pl.pallas_call(
        partial(kernel, n_seq, n_tp, heads * n_tp * WIDTH),
        out_shape=(
            jax.ShapeDtypeStruct(x.shape, bf16),
            jax.ShapeDtypeStruct(q.shape, bf16),
        ),
        in_specs=[pl.BlockSpec(memory_space=pltpu.SMEM)] + [vmem] * 9,
        out_specs=(vmem, vmem),
        scratch_shapes=[
            pltpu.VMEM((CYCLE, 2) + k.shape, bf16),
            pltpu.VMEM((CYCLE + 1, rows, rows), f32),
            pltpu.VMEM((heads, 1, rows), f32),
            pltpu.VMEM((heads, rows, WIDTH), f32),
            pltpu.VMEM((WIDTH, rows), bf16),
            pltpu.VMEM((2, BLOCK, BLOCK), f32),
            pltpu.VMEM(x.shape, f32),
            states, states, states, states, states, states,
            pltpu.VMEM((heads, 1, WIDTH), f32),
            pltpu.VMEM((heads, 1, WIDTH), f32),
            pltpu.VMEM((rows, WIDTH), f32),
            pltpu.VMEM((8, rows), f32),
            pltpu.VMEM((n_tp - 1, 8, rows), f32),
            dma((5, 2)), dma((CYCLE, 2)),
            dma((chunks,)), dma((chunks,)), dma((chunks,)), dma((chunks,)), dma((chunks,)),
            dma((2,)), dma((n_tp - 1,)), dma((n_tp - 1,)),
        ],
        compiler_params=pltpu.CompilerParams(
            collective_id=0, has_side_effects=True, vmem_limit_bytes=60 * 1024 * 1024
        ),
    )(request_blocks, x, gate, write, read, decay, gain.reshape(1, -1), q, k, v)


def solution(mesh):
    placed = (
        P("seq", "tp"),
        P("seq", "tp"),
        P("seq", None),
        P("seq", None),
        P("tp", "seq"),
        P("tp"),
        P("seq", "tp"),
        P("seq", "tp"),
        P("seq", "tp"),
        P(),
    )
    return jax.shard_map(
        partial(on_device, mesh.shape["seq"], mesh.shape["tp"]),
        mesh=mesh,
        in_specs=placed,
        out_specs=(P("seq", "tp"), P("seq", "tp")),
        check_vma=False,
    )
```

time: 215 us -> 85.9 us (0.40)
  the two profiles are of different devices: /device:TPU:26 before, /device:TPU:29 now
where the time goes in v1:
time: 85.9 us; the launch traced here: 85.7 us
  Pallas kernels  80.9 us (94%)
  local copies, waits for them, and re-layouts  4.19 us (5%)
    pallas_call x1, Pallas kernels, on_device(): pl.pallas_call(partial(kernel, n_seq, n_tp, heads * n_tp * WIDTH), out_sh...  80.9 us
    unnamed x4, local copies, waits for them, and re-layouts  4.19 us

profile of v1, /device:TPU:29, one launch (start us, length us, event | category | flops | bytes accessed | tf_op | source)
XLA Modules:
  0.0 85.7 jit_solution(914572191565178041)
XLA Ops:
  0.6 80.9 %shard_map.113 = (bf16[256,4096]{1,0:T(8,128)(2,1)}, bf16[256,2048]{1,0:T(8,128)(2,1)}) custom-call(s32[4]{0:T(128)} %rb.1, bf16[256,4096]{1,0:T(8,128)(2,1)} %x_ref.1, bf16[256,4096]{1,0:T(8,128)(2,1)} %g_ref.1, bf16[256,128]{1,0:T(8,128)(2,1)} %b_ref.1, bf16[256,128]{1,0:T(8,128)(2,1)} %c_ref.1, f32[32,256]{1,0:T(8,128)} %ld_ref.1, f32[1,4096]{1,0:T(1,128)} %bitcast.1, ...), custom_call_target="tpu_custom_call" | custom-call | tf_op jit(solution)/shard_map/pallas_call | solution.py:408
  81.5 0.0 copy-start
  81.5 3.2 %copy.14 = bf16[256,4096]{1,0:T(8,128)(2,1)} copy(bf16[256,4096]{1,0:T(8,128)(2,1)} %get-tuple-element.4) | data formatting | bytes 4194304
  84.7 0.0 copy-done
  84.7 1.0 %copy.15 = bf16[256,2048]{1,0:T(8,128)(2,1)} copy(bf16[256,2048]{1,0:T(8,128)(2,1)S(1)} %copy-done) | data formatting | bytes 2097152
Async XLA Ops:
  81.5 3.2 %copy-start = (bf16[256,2048]{1,0:T(8,128)(2,1)S(1)}, bf16[256,2048]{1,0:T(8,128)(2,1)}, u32[]{:S(2)}) copy-start(bf16[256,2048]{1,0:T(8,128)(2,1)} %get-tuple-element.5) | copy-start | bytes 3145732

commit v2 on v1

--- a/solution.py
+++ b/solution.py
@@ -11,7 +11,7 @@
 WIDTH = 128
 BLOCK = 128
 CYCLE = 4
-CHUNK = 4
+CHUNK = 2
 FAR = -1e30
 MESH = pl.DeviceIdType.MESH
 HIGH = lax.Precision.HIGHEST
@@ -35,9 +35,9 @@
     n_seq, n_tp, features,
     rb, x_ref, g_ref, b_ref, c_ref, ld_ref, gain_ref, q_ref, k_ref, v_ref,
     out_ref, att_ref,
-    kv, bias, run, colb, bt, aff, wbuf, s0, slab, partner_s, ent, ent_own, eout,
-    gdec, gpart, sq, ss, ssbuf,
-    kv_send, kv_recv, st_send, st_recv, ev_send, e_recv, ch_send, gd_sem, ss_send, ss_recv,
+    kv, bias, run, colb, bt, aff, wbuf, s0, slab, partner_s, ent, ent_own, eout, eside,
+    acc, tops, sums_of, gdec, gpart, sq, ss, ssbuf,
+    kv_send, kv_recv, st_send, st_recv, ev_send, e_recv, ch_send, c_recv, gd_sem, ss_send, ss_recv,
 ):
     d = lax.axis_index("seq")
     t = lax.axis_index("tp")
@@ -52,7 +52,9 @@
     q_heads = q_ref.shape[1] // WIDTH
     kv_heads = k_ref.shape[1] // WIDTH
     group = q_heads // kv_heads
-    chunks = heads // CHUNK
+    near = heads // CHUNK // 2
+    mine = odd * near
+    theirs = near - mine
     half = (slice(0, BLOCK), slice(BLOCK, 2 * BLOCK))
 
     barrier = pltpu.get_barrier_semaphore()
@@ -116,9 +118,15 @@
         def _():
             kv[slot] = jnp.zeros(kv.shape[1:], kv.dtype)
 
+    span = near * CHUNK
+
     @pl.when(d < 2)
     def _():
-        ent[...] = jnp.zeros(ent.shape, ent.dtype)
+        ent[pl.ds(mine * CHUNK, span)] = jnp.zeros((span,) + ent.shape[1:], ent.dtype)
+
+    @pl.when((d < 2) & is_even)
+    def _():
+        ent_own[pl.ds(theirs * CHUNK, span)] = jnp.zeros((span,) + ent.shape[1:], ent.dtype)
 
     ends = []
     total = jnp.int32(0)
@@ -155,10 +163,7 @@
             device_id={"seq": partner}, device_id_type=MESH,
         )
 
-    @pl.when(is_even)
-    def _():
-        decay_copy().start()
-
+    decay_copy().start()
     bt[...] = b_ref[...].astype(jnp.float32).T.astype(jnp.bfloat16)
 
     def part_of(ref, c):
@@ -171,17 +176,17 @@
             device_id={"seq": partner}, device_id_type=MESH,
         )
 
-    def side_copy(c):
+    def side_copy(c, source):
         return pltpu.make_async_remote_copy(
-            src_ref=part_of(ent, c), dst_ref=part_of(ent, c),
+            src_ref=part_of(source, c), dst_ref=part_of(ent_own, c),
             send_sem=ev_send.at[c], recv_sem=e_recv.at[c],
-            device_id={"seq": d - 1}, device_id_type=MESH,
+            device_id={"seq": partner}, device_id_type=MESH,
         )
 
     def chain_copy(c):
         return pltpu.make_async_remote_copy(
             src_ref=part_of(eout, c), dst_ref=part_of(ent, c),
-            send_sem=ch_send.at[c], recv_sem=e_recv.at[c],
+            send_sem=ch_send.at[c], recv_sem=c_recv.at[c],
             device_id={"seq": d + 2}, device_id_type=MESH,
         )
 
@@ -196,17 +201,20 @@
         s0[h] = states[0].astype(jnp.bfloat16)
         slab[h] = (g_1 * states[0] + states[1]).astype(jnp.bfloat16)
 
-    def state_chunk(c, carry):
-        for i in range(CHUNK):
-            state_of(c * CHUNK + i)
-
-        @pl.when(is_even)
-        def _():
-            slab_copy(c).start()
-
-        return carry
-
-    lax.fori_loop(0, chunks, state_chunk, 0)
+    def state_sent(i, carry):
+        c = theirs + i
+        for j in range(CHUNK):
+            state_of(c * CHUNK + j)
+        slab_copy(c).start()
+        return carry
+
+    def state_kept(i, carry):
+        for j in range(CHUNK):
+            state_of((mine + i) * CHUNK + j)
+        return carry
+
+    lax.fori_loop(0, near, state_sent, 0)
+    lax.fori_loop(0, near, state_kept, 0)
 
     arrived(1)
     start(relay_up)
@@ -219,15 +227,68 @@
         jnp.int32, (BLOCK, BLOCK), 0
     )
 
-    def within_of(h, carry):
+    def within_of(h):
         for b in range(2):
             spread = colb[h, half[b], :] - run[h, :, half[b]]
             weight = jnp.exp(jnp.where(causal, spread, FAR))
             mixing = (weight * aff[b]).astype(jnp.bfloat16)
             wbuf[half[b], lanes(h)] = dot(mixing, x_ref[half[b], lanes(h)])
-        return carry
-
-    lax.fori_loop(0, heads, within_of, 0)
+
+    def relay(c):
+        slab_copy(c).wait_recv()
+
+        @pl.when(has_prev)
+        def _():
+            chain_copy(c).wait_recv()
+
+        @pl.when(is_odd)
+        def _():
+            @pl.when(has_prev)
+            def _():
+                side_copy(c, ent).start()
+
+            for i in range(CHUNK):
+                h = c * CHUNK + i
+                own = gpart[h] * ent[h].astype(jnp.float32) + partner_s[h].astype(jnp.float32)
+                ent_own[h] = own.astype(jnp.bfloat16)
+                eout[h] = (gdec[h] * own + slab[h].astype(jnp.float32)).astype(jnp.bfloat16)
+
+        @pl.when(is_even)
+        def _():
+            for i in range(CHUNK):
+                h = c * CHUNK + i
+                ent_own[h] = ent[h]
+                after = gdec[h] * ent[h].astype(jnp.float32) + slab[h].astype(jnp.float32)
+                eside[h] = after.astype(jnp.bfloat16)
+                eout[h] = (gpart[h] * after + partner_s[h].astype(jnp.float32)).astype(
+                    jnp.bfloat16
+                )
+            side_copy(c, eside).start()
+
+        @pl.when(has_next)
+        def _():
+            chain_copy(c).start()
+
+    offset = jnp.minimum(d // 2 * 2 + 1, near)
+
+    def relay_at(step):
+        c = step - offset
+
+        @pl.when((c >= 0) & (c < near))
+        def _():
+            relay(mine + c)
+
+    decay_copy().wait_recv()
+
+    per_within = heads // near
+
+    def within_step(i, carry):
+        for j in range(per_within):
+            within_of(i * per_within + j)
+        relay_at(i)
+        return carry
+
+    lax.fori_loop(0, near, within_step, 0)
 
     def label(positions):
         found = jnp.zeros(positions.shape, jnp.int32)
@@ -242,72 +303,69 @@
         same = (q_label == label(k_pos)) & (k_pos <= q_pos)
         bias[slot] = jnp.where(same, 0.0, FAR)
 
-    arrived(3)
-    start(last_odd)
-    arrived(0)
-    arrived(2)
-
-    @pl.when(is_odd)
-    def _():
-        decay_copy().wait_recv()
-
     factor = math.log2(math.e) / math.sqrt(WIDTH)
-
-    def attend(h):
+    per = q_heads // near
+
+    def partial_of(h, slots):
         kh = h // group
         query = q_ref[:, lanes(h)]
         scores = []
-        for slot in range(CYCLE + 1):
+        for slot in slots:
             key = k_ref[:, lanes(kh)] if slot == 0 else kv[slot - 1, 0, :, lanes(kh)]
             scores.append(dot_t(query, key) + bias[slot])
         top = scores[0]
         for s in scores[1:]:
             top = jnp.maximum(top, s)
         top = jnp.max(top, axis=1, keepdims=True)
-        sums = jnp.zeros((rows, rows), jnp.float32)
+        return scores, top
+
+    def weigh(h, slots, scores, top):
+        kh = h // group
+        total = jnp.zeros((rows, rows), jnp.float32)
         result = jnp.zeros((rows, WIDTH), jnp.float32)
-        for slot in range(CYCLE + 1):
+        for slot, s in zip(slots, scores):
             value = v_ref[:, lanes(kh)] if slot == 0 else kv[slot - 1, 1, :, lanes(kh)]
-            weight = jnp.exp2((scores[slot] - top) * factor)
-            sums = sums + weight
+            weight = jnp.exp2((s - top) * factor)
+            total = total + weight
             result = result + dot(weight.astype(jnp.bfloat16), value)
-        result = result / jnp.sum(sums, axis=1, keepdims=True)
-        att_ref[:, lanes(h)] = result.astype(jnp.bfloat16)
-
-    def relay(c):
-        slab_copy(c).wait_recv()
-
-        @pl.when(has_prev)
-        def _():
-            chain_copy(c).wait_recv()
-            side_copy(c).start()
-
-        for i in range(CHUNK):
-            h = c * CHUNK + i
-            own = gpart[h] * ent[h].astype(jnp.float32) + partner_s[h].astype(
-                jnp.float32
-            )
-            ent_own[h] = own.astype(jnp.bfloat16)
-            after = gdec[h] * own + slab[h].astype(jnp.float32)
-            eout[h] = after.astype(jnp.bfloat16)
-
-        @pl.when(has_next)
-        def _():
-            chain_copy(c).start()
-
-    per = q_heads // chunks
-
-    def both(c, carry):
-        for i in range(per):
-            attend(c * per + i)
-
-        @pl.when(is_odd)
-        def _():
-            relay(c)
-
-        return carry
-
-    lax.fori_loop(0, chunks, both, 0)
+        return jnp.sum(total, axis=1, keepdims=True), result
+
+    first = (0, 2, 4)
+    second = (1, 3)
+
+    def attend_first(h):
+        scores, top = partial_of(h, first)
+        total, result = weigh(h, first, scores, top)
+        tops[h] = jnp.broadcast_to(top, (rows, WIDTH))
+        sums_of[h] = jnp.broadcast_to(total, (rows, WIDTH))
+        acc[h] = result
+
+    def attend_second(h):
+        scores, top = partial_of(h, second)
+        before = tops[h]
+        top = jnp.maximum(jnp.broadcast_to(top, (rows, WIDTH)), before)
+        shrink = jnp.exp2((before - top) * factor)
+        total, result = weigh(h, second, scores, top[:, :1])
+        total = sums_of[h] * shrink + total
+        att_ref[:, lanes(h)] = ((acc[h] * shrink + result) / total).astype(jnp.bfloat16)
+
+    def first_step(i, carry):
+        for j in range(per):
+            attend_first(i * per + j)
+        relay_at(near + i)
+        return carry
+
+    def second_step(i, carry):
+        for j in range(per):
+            attend_second(i * per + j)
+        return carry
+
+    arrived(3)
+    start(last_odd)
+    lax.fori_loop(0, near, first_step, 0)
+    arrived(0)
+    arrived(2)
+    lax.fori_loop(0, near, second_step, 0)
 
     sq[...] = jnp.zeros(sq.shape, jnp.float32)
 
@@ -325,20 +383,24 @@
             wbuf[half[b], lanes(h)] = gated
             sq[half[b], :] = sq[half[b], :] + gated * gated
 
-    def finish(c, carry):
-        @pl.when(is_even)
-        def _():
-            @pl.when(has_prev)
-            def _():
-                side_copy(c).wait_recv()
-
-            ent_own[pl.ds(c * CHUNK, CHUNK)] = ent[pl.ds(c * CHUNK, CHUNK)]
-
-        for i in range(CHUNK):
-            finish_of(c * CHUNK + i)
-        return carry
-
-    lax.fori_loop(0, chunks, finish, 0)
+    def finish_mine(i, carry):
+        for j in range(CHUNK):
+            finish_of((mine + i) * CHUNK + j)
+        return carry
+
+    def finish_theirs(i, carry):
+        c = theirs + i
+
+        @pl.when(is_odd | has_prev)
+        def _():
+            side_copy(c, ent).wait_recv()
+
+        for j in range(CHUNK):
+            finish_of(c * CHUNK + j)
+        return carry
+
+    lax.fori_loop(0, near, finish_mine, 0)
+    lax.fori_loop(0, near, finish_theirs, 0)
 
     ss[...] = dot_t(jnp.ones((8, WIDTH), jnp.float32), sq[...], HIGH)
 
@@ -374,26 +436,22 @@
     for move in (own_up, own_side, relay_up, relay_even, relay_odd, last_odd):
         sent(move)
 
-    @pl.when(is_even)
-    def _():
-        decay_copy().wait_send()
-
-    def drain(c, carry):
-        @pl.when(is_even)
-        def _():
-            slab_copy(c).wait_send()
-
-        @pl.when(is_odd & has_prev)
-        def _():
-            side_copy(c).wait_send()
-
-        @pl.when(is_odd & has_next)
-        def _():
-            chain_copy(c).wait_send()
-
-        return carry
-
-    lax.fori_loop(0, chunks, drain, 0)
+    decay_copy().wait_send()
+
+    def drain(i, carry):
+        slab_copy(theirs + i).wait_send()
+
+        @pl.when(is_even | has_prev)
+        def _():
+            side_copy(mine + i, ent).wait_send()
+
+        @pl.when(has_next)
+        def _():
+            chain_copy(mine + i).wait_send()
+
+        return carry
+
+    lax.fori_loop(0, near, drain, 0)
 
 
 def on_device(n_seq, n_tp, *args):
@@ -403,6 +461,7 @@
     chunks = heads // CHUNK
     f32, bf16 = jnp.float32, jnp.bfloat16
     states = pltpu.VMEM((heads, WIDTH, WIDTH), bf16)
+    softmax = pltpu.VMEM((q.shape[1] // WIDTH, rows, WIDTH), f32)
     dma = pltpu.SemaphoreType.DMA
     vmem = pl.BlockSpec(memory_space=pltpu.VMEM)
     return pl.pallas_call(
@@ -421,7 +480,8 @@
             pltpu.VMEM((WIDTH, rows), bf16),
             pltpu.VMEM((2, BLOCK, BLOCK), f32),
             pltpu.VMEM(x.shape, f32),
-            states, states, states, states, states, states,
+            states, states, states, states, states, states, states,
+            softmax, softmax, softmax,
             pltpu.VMEM((heads, 1, WIDTH), f32),
             pltpu.VMEM((heads, 1, WIDTH), f32),
             pltpu.VMEM((rows, WIDTH), f32),
@@ -429,6 +489,7 @@
             pltpu.VMEM((n_tp - 1, 8, rows), f32),
             dma((5, 2)), dma((CYCLE, 2)),
             dma((chunks,)), dma((chunks,)), dma((chunks,)), dma((chunks,)), dma((chunks,)),
+            dma((chunks,)),
             dma((2,)), dma((n_tp - 1,)), dma((n_tp - 1,)),
         ],
         compiler_params=pltpu.CompilerParams(

time: 85.9 us -> 61.1 us (0.71)
  the two profiles are of different devices: /device:TPU:29 before, /device:TPU:17 now
where the time goes in v2:
time: 61.1 us; the launch traced here: 60.9 us
  Pallas kernels  56.1 us (92%)
  local copies, waits for them, and re-layouts  4.19 us (7%)
  between operations  0.65 us (1%)
    pallas_call x1, Pallas kernels, on_device(): pl.pallas_call(partial(kernel, n_seq, n_tp, heads * n_tp * WIDTH), out_sh...  56.1 us
    unnamed x4, local copies, waits for them, and re-layouts  4.19 us

profile of v2, /device:TPU:17, one launch (start us, length us, event | category | flops | bytes accessed | tf_op | source)
XLA Modules:
  0.0 60.9 jit_solution(3215290811830537368)
XLA Ops:
  0.6 56.1 %shard_map.113 = (bf16[256,4096]{1,0:T(8,128)(2,1)}, bf16[256,2048]{1,0:T(8,128)(2,1)}) custom-call(s32[4]{0:T(128)} %rb.1, bf16[256,4096]{1,0:T(8,128)(2,1)} %x_ref.1, bf16[256,4096]{1,0:T(8,128)(2,1)} %g_ref.1, bf16[256,128]{1,0:T(8,128)(2,1)} %b_ref.1, bf16[256,128]{1,0:T(8,128)(2,1)} %c_ref.1, f32[32,256]{1,0:T(8,128)} %ld_ref.1, f32[1,4096]{1,0:T(1,128)} %bitcast.1, ...), custom_call_target="tpu_custom_call" | custom-call | tf_op jit(solution)/shard_map/pallas_call | solution.py:467
  56.7 0.0 copy-start
  56.8 3.2 %copy.14 = bf16[256,4096]{1,0:T(8,128)(2,1)} copy(bf16[256,4096]{1,0:T(8,128)(2,1)} %get-tuple-element.4) | data formatting | bytes 4194304
  60.0 0.0 copy-done
  60.0 1.0 %copy.15 = bf16[256,2048]{1,0:T(8,128)(2,1)} copy(bf16[256,2048]{1,0:T(8,128)(2,1)S(1)} %copy-done) | data formatting | bytes 2097152
Async XLA Ops:
  56.7 3.2 %copy-start = (bf16[256,2048]{1,0:T(8,128)(2,1)S(1)}, bf16[256,2048]{1,0:T(8,128)(2,1)}, u32[]{:S(2)}) copy-start(bf16[256,2048]{1,0:T(8,128)(2,1)} %get-tuple-element.5) | copy-start | bytes 3145732

commit v3 on v2

--- a/solution.py
+++ b/solution.py
@@ -33,11 +33,11 @@
 
 def kernel(
     n_seq, n_tp, features,
-    rb, x_ref, g_ref, b_ref, c_ref, ld_ref, gain_ref, q_ref, k_ref, v_ref,
-    out_ref, att_ref,
-    kv, bias, run, colb, bt, aff, wbuf, s0, slab, partner_s, ent, ent_own, eout, eside,
-    acc, tops, sums_of, gdec, gpart, sq, ss, ssbuf,
-    kv_send, kv_recv, st_send, st_recv, ev_send, e_recv, ch_send, c_recv, gd_sem, ss_send, ss_recv,
+    rb, x_ref, g_ref, b_ref, c_ref, ld_ref, q_ref, k_ref, v_ref,
+    wbuf, att_ref, scale_ref,
+    kv, bias, run, colb, bt, aff, s0, slab, partner_s, ent, ent_own, eout, eside,
+    acc, tops, masks, q_vm, g_vm, gdec, gpart, sq, ss, ssbuf,
+    load_sem, kv_send, kv_recv, st_send, st_recv, ev_send, e_recv, ch_send, c_recv, gd_sem, ss_send, ss_recv,
 ):
     d = lax.axis_index("seq")
     t = lax.axis_index("tp")
@@ -57,6 +57,11 @@
     theirs = near - mine
     half = (slice(0, BLOCK), slice(BLOCK, 2 * BLOCK))
 
+    q_load = pltpu.make_async_copy(q_ref, q_vm, load_sem.at[0])
+    g_load = pltpu.make_async_copy(g_ref, g_vm, load_sem.at[1])
+    q_load.start()
+    g_load.start()
+
     barrier = pltpu.get_barrier_semaphore()
     pl.semaphore_signal(barrier, inc=1, device_id={"seq": partner}, device_id_type=MESH)
     for r in range(1, n_tp):
@@ -297,57 +302,66 @@
         return jnp.where(positions < 0, -1, found)
 
     q_pos = d * rows + lax.broadcasted_iota(jnp.int32, (rows, 1), 0)
-    q_label = label(q_pos)
-    for slot in range(CYCLE + 1):
-        k_pos = (d - slot) * rows + lax.broadcasted_iota(jnp.int32, (1, rows), 1)
-        same = (q_label == label(k_pos)) & (k_pos <= q_pos)
-        bias[slot] = jnp.where(same, 0.0, FAR)
-
+    own_pos = d * rows + lax.broadcasted_iota(jnp.int32, (1, rows), 1)
+    bias[...] = jnp.where((label(q_pos) == label(own_pos)) & (own_pos <= q_pos), 0.0, FAR)
+    line = lax.broadcasted_iota(jnp.int32, (rows, WIDTH), 0)
+    lane = lax.broadcasted_iota(jnp.int32, (rows, WIDTH), 1)
+    lane_label = label(d * rows + jnp.minimum(lane, 1) * BLOCK)
+    select = jnp.where(lane == line // BLOCK, 1.0, 0.0).astype(jnp.bfloat16)
+    ones = jnp.ones((rows, WIDTH), jnp.bfloat16)
+    for slot in range(1, CYCLE + 1):
+        other = label((d - slot) * rows + line) != lane_label
+        masks[slot - 1] = jnp.where(other & (lane < 2), FAR, 0.0).astype(jnp.bfloat16)
+
+    q_load.wait()
     factor = math.log2(math.e) / math.sqrt(WIDTH)
     per = q_heads // near
 
-    def partial_of(h, slots):
+    def twice(a):
+        return jnp.concatenate([a, a], axis=1)
+
+    def scores_of(h, slots):
         kh = h // group
-        query = q_ref[:, lanes(h)]
+        query = q_vm[:, lanes(h)]
+        wide = jnp.concatenate([query, select], axis=1)
         scores = []
         for slot in slots:
-            key = k_ref[:, lanes(kh)] if slot == 0 else kv[slot - 1, 0, :, lanes(kh)]
-            scores.append(dot_t(query, key) + bias[slot])
+            if slot == 0:
+                scores.append(dot_t(query, k_ref[:, lanes(kh)]) + bias[...])
+            else:
+                key = jnp.concatenate([kv[slot - 1, 0, :, lanes(kh)], masks[slot - 1]], axis=1)
+                scores.append(dot_t(wide, key))
         top = scores[0]
         for s in scores[1:]:
             top = jnp.maximum(top, s)
         top = jnp.max(top, axis=1, keepdims=True)
-        return scores, top
+        return scores, jnp.broadcast_to(top, (rows, WIDTH))
 
     def weigh(h, slots, scores, top):
         kh = h // group
-        total = jnp.zeros((rows, rows), jnp.float32)
-        result = jnp.zeros((rows, WIDTH), jnp.float32)
+        result = None
         for slot, s in zip(slots, scores):
             value = v_ref[:, lanes(kh)] if slot == 0 else kv[slot - 1, 1, :, lanes(kh)]
-            weight = jnp.exp2((s - top) * factor)
-            total = total + weight
-            result = result + dot(weight.astype(jnp.bfloat16), value)
-        return jnp.sum(total, axis=1, keepdims=True), result
+            weight = jnp.exp2((s - twice(top)) * factor).astype(jnp.bfloat16)
+            part = dot(weight, jnp.concatenate([value, ones], axis=1))
+            result = part if result is None else result + part
+        return result
 
     first = (0, 2, 4)
     second = (1, 3)
 
     def attend_first(h):
-        scores, top = partial_of(h, first)
-        total, result = weigh(h, first, scores, top)
-        tops[h] = jnp.broadcast_to(top, (rows, WIDTH))
-        sums_of[h] = jnp.broadcast_to(total, (rows, WIDTH))
-        acc[h] = result
+        scores, top = scores_of(h, first)
+        tops[h] = top
+        acc[h] = weigh(h, first, scores, top)
 
     def attend_second(h):
-        scores, top = partial_of(h, second)
+        scores, top = scores_of(h, second)
         before = tops[h]
-        top = jnp.maximum(jnp.broadcast_to(top, (rows, WIDTH)), before)
+        top = jnp.maximum(top, before)
         shrink = jnp.exp2((before - top) * factor)
-        total, result = weigh(h, second, scores, top[:, :1])
-        total = sums_of[h] * shrink + total
-        att_ref[:, lanes(h)] = ((acc[h] * shrink + result) / total).astype(jnp.bfloat16)
+        result = acc[h] * twice(shrink) + weigh(h, second, scores, top)
+        att_ref[:, lanes(h)] = (result[:, :WIDTH] / result[:, WIDTH:]).astype(jnp.bfloat16)
 
     def first_step(i, carry):
         for j in range(per):
@@ -378,8 +392,8 @@
             from_state = dot(c_ref[half[b], :], states[b])
             entry = opens[b] * jnp.exp(colb[h, half[b], :])
             mixed = wbuf[half[b], lanes(h)] + from_state * entry
-            gate = g_ref[half[b], lanes(h)].astype(jnp.float32)
-            gated = mixed * (gate / (1.0 + jnp.exp(-gate)))
+            gate = 0.5 * g_vm[half[b], lanes(h)].astype(jnp.float32)
+            gated = mixed * (gate + gate * jnp.tanh(gate))
             wbuf[half[b], lanes(h)] = gated
             sq[half[b], :] = sq[half[b], :] + gated * gated
 
@@ -399,6 +413,7 @@
             finish_of(c * CHUNK + j)
         return carry
 
+    g_load.wait()
     lax.fori_loop(0, near, finish_mine, 0)
     lax.fori_loop(0, near, finish_theirs, 0)
 
@@ -421,15 +436,7 @@
         squares, jnp.full((8, WIDTH), 0.125, jnp.float32), (((0,), (0,)), ((), ())),
         preferred_element_type=jnp.float32, precision=HIGH,
     )
-    sq[...] = lax.rsqrt(spread_out / features + 1e-05)
-
-    def scale_out(h, carry):
-        out_ref[:, lanes(h)] = (
-            wbuf[:, lanes(h)] * sq[...] * gain_ref[:, lanes(h)]
-        ).astype(jnp.bfloat16)
-        return carry
-
-    lax.fori_loop(0, heads, scale_out, 0)
+    scale_ref[...] = lax.rsqrt(spread_out / features + 1e-05)
 
     for r in range(1, n_tp):
         squares_copy(r).wait_send()
@@ -464,30 +471,32 @@
     softmax = pltpu.VMEM((q.shape[1] // WIDTH, rows, WIDTH), f32)
     dma = pltpu.SemaphoreType.DMA
     vmem = pl.BlockSpec(memory_space=pltpu.VMEM)
-    return pl.pallas_call(
+    hbm = pl.BlockSpec(memory_space=pl.ANY)
+    gated, attention, scale = pl.pallas_call(
         partial(kernel, n_seq, n_tp, heads * n_tp * WIDTH),
         out_shape=(
-            jax.ShapeDtypeStruct(x.shape, bf16),
+            jax.ShapeDtypeStruct(x.shape, f32),
             jax.ShapeDtypeStruct(q.shape, bf16),
+            jax.ShapeDtypeStruct((rows, WIDTH), f32),
         ),
-        in_specs=[pl.BlockSpec(memory_space=pltpu.SMEM)] + [vmem] * 9,
-        out_specs=(vmem, vmem),
+        in_specs=[pl.BlockSpec(memory_space=pltpu.SMEM), vmem, hbm, vmem, vmem, vmem, hbm, vmem, vmem],
+        out_specs=(vmem, vmem, vmem),
         scratch_shapes=[
             pltpu.VMEM((CYCLE, 2) + k.shape, bf16),
-            pltpu.VMEM((CYCLE + 1, rows, rows), f32),
+            pltpu.VMEM((rows, rows), f32),
             pltpu.VMEM((heads, 1, rows), f32),
             pltpu.VMEM((heads, rows, WIDTH), f32),
             pltpu.VMEM((WIDTH, rows), bf16),
             pltpu.VMEM((2, BLOCK, BLOCK), f32),
-            pltpu.VMEM(x.shape, f32),
             states, states, states, states, states, states, states,
-            softmax, softmax, softmax,
+            pltpu.VMEM((q.shape[1] // WIDTH, rows, 2 * WIDTH), f32), softmax,
+            pltpu.VMEM((CYCLE, rows, WIDTH), bf16), pltpu.VMEM(q.shape, bf16), pltpu.VMEM(x.shape, bf16),
             pltpu.VMEM((heads, 1, WIDTH), f32),
             pltpu.VMEM((heads, 1, WIDTH), f32),
             pltpu.VMEM((rows, WIDTH), f32),
             pltpu.VMEM((8, rows), f32),
             pltpu.VMEM((n_tp - 1, 8, rows), f32),
-            dma((5, 2)), dma((CYCLE, 2)),
+            dma((2,)), dma((5, 2)), dma((CYCLE, 2)),
             dma((chunks,)), dma((chunks,)), dma((chunks,)), dma((chunks,)), dma((chunks,)),
             dma((chunks,)),
             dma((2,)), dma((n_tp - 1,)), dma((n_tp - 1,)),
@@ -495,7 +504,9 @@
         compiler_params=pltpu.CompilerParams(
             collective_id=0, has_side_effects=True, vmem_limit_bytes=60 * 1024 * 1024
         ),
-    )(request_blocks, x, gate, write, read, decay, gain.reshape(1, -1), q, k, v)
+    )(request_blocks, x, gate, write, read, decay, q, k, v)
+    out = gated * scale[:, :1] * gain[None, :]
+    return out.astype(bf16), attention
 
 
 def solution(mesh):

time: 61.1 us -> 59.7 us (0.977)
  other arithmetic: 0 us -> 4.09 us
  Pallas kernels: 56.1 us -> 52.6 us
  local copies, waits for them, and re-layouts: 4.19 us -> 2.07 us
    convert_element_type x0 -> x1, other arithmetic: none -> 4.09 us  [on_device(): return (out.astype(bf16), attention)]
    pallas_call x1, Pallas kernels: 56.1 us -> 52.6 us  [on_device(): pl.pallas_call(partial(kernel, n_seq, n_tp, heads * n_tp * WIDTH), out_sh...]
    unnamed x4 -> x5, local copies, waits for them, and re-layouts: 4.19 us -> 0.98 us
    slice x0 -> x1, local copies, waits for them, and re-layouts: none -> 1.09 us  [on_device(): out = gated * scale[:, :1] * gain[None, :]]
where the time goes in v3:
time: 59.7 us; the launch traced here: 59.5 us
  Pallas kernels  52.6 us (88%)
  other arithmetic  4.09 us (7%)
  local copies, waits for them, and re-layouts  2.07 us (3%)
  between operations  0.67 us (1%)
    pallas_call x1, Pallas kernels, on_device(): pl.pallas_call(partial(kernel, n_seq, n_tp, heads * n_tp * WIDTH), out_sh...  52.6 us
    convert_element_type x1, other arithmetic, on_device(): return (out.astype(bf16), attention)  4.09 us

profile of v3, /device:TPU:17, one launch (start us, length us, event | category | flops | bytes accessed | tf_op | source)
XLA Modules:
  0.0 59.5 jit_solution(11433094806051500695)
XLA Ops:
  0.6 0.0 copy-start.1
  0.6 52.6 %shard_map.113 = (f32[256,4096]{1,0:T(8,128)}, bf16[256,2048]{1,0:T(8,128)(2,1)}, f32[256,128]{1,0:T(8,128)}) custom-call(s32[4]{0:T(128)} %rb.1, bf16[256,4096]{1,0:T(8,128)(2,1)} %x_ref.1, bf16[256,4096]{1,0:T(8,128)(2,1)} %g_ref.1, bf16[256,128]{1,0:T(8,128)(2,1)} %b_ref.1, bf16[256,128]{1,0:T(8,128)(2,1)} %c_ref.1, f32[32,256]{1,0:T(8,128)} %ld_ref.1, ...), custom_call_target="tpu_custom_call" | custom-call | tf_op jit(solution)/shard_map/pallas_call | solution.py:475
  53.3 0.0 copy-start
  53.3 1.1 %slice_reduce_fusion = f32[256]{0:T(256)S(1)} fusion(f32[256,128]{1,0:T(8,128)} %get-tuple-element.6), kind=kLoop, calls=%fused_computation.1 | loop fusion | bytes 2048 | tf_op jit(solution)/shard_map/slice | solution.py:508
  54.4 0.0 copy-done.1
  54.4 4.1 %multiply_convert_fusion = bf16[256,4096]{1,0:T(8,128)(2,1)} fusion(f32[256,4096]{1,0:T(8,128)} %get-tuple-element.5, f32[4096]{0:T(1024)S(1)} %copy-done.1, f32[256]{0:T(256)S(1)} %slice_reduce_fusion), kind=kLoop, calls=%fused_computation | loop fusion | flops 3145728 | bytes 6308864 | tf_op jit(solution)/shard_map/convert_element_type | solution.py:509
  58.5 0.0 copy-done
  58.5 1.0 %copy.13 = bf16[256,2048]{1,0:T(8,128)(2,1)} copy(bf16[256,2048]{1,0:T(8,128)(2,1)S(1)} %copy-done) | data formatting | bytes 2097152
Async XLA Ops:
  0.6 53.8 %copy-start.1 = (f32[4096]{0:T(1024)S(1)}, f32[4096]{0:T(1024)}, u32[]{:S(2)}) copy-start(f32[4096]{0:T(1024)} %param.15) | copy-start | bytes 49156
  53.3 5.2 %copy-start = (bf16[256,2048]{1,0:T(8,128)(2,1)S(1)}, bf16[256,2048]{1,0:T(8,128)(2,1)}, u32[]{:S(2)}) copy-start(bf16[256,2048]{1,0:T(8,128)(2,1)} %get-tuple-element.11) | copy-start | bytes 3145732
